TPU v7x, 32 devices: a whole 2x2x4 slice. The times are simulated.
32 devices in a mesh: dp: 2 (over y), row: 4 (over x, core), col: 4 (over z).
Axes of the slice: x: 2, y: 2, z: 4, core: 2. Of those that a mesh axis runs over, the one named last changes fastest.
Arguments:
- features: bfloat16 [2, 32, 512, 256], P('dp', 'row', 'col'), may hold values from -6 to 6
- reduce_weight: bfloat16 [256, 128], replicated, may hold values from -0.375 to 0.375
- scale_one: float32 [128], replicated, may hold values from 0.25 to 1.75
- shift_one: float32 [128], replicated, may hold values from -3 to 3
- group_weight: bfloat16 [3, 3, 4, 128], replicated, may hold values from -1 to 1
- scale_two: float32 [128], replicated, may hold values from 0.25 to 1.75
- shift_two: float32 [128], replicated, may hold values from -3 to 3
- expand_weight: bfloat16 [128, 256], replicated, may hold values from -0.5 to 0.5
- scale_three: float32 [256], replicated, may hold values from 0.25 to 1.75
- shift_three: float32 [256], replicated, may hold values from -3 to 3
- cotangent: bfloat16 [2, 32, 512, 256], P('dp', 'row', 'col'), may hold values from -6 to 6
Outputs:
- input_grad: bfloat16 [2, 32, 512, 256], P('dp', 'row', 'col')
- reduce_grad: float32 [256, 128], P('dp')
- group_grad: float32 [128, 3, 3, 4], P('dp')
- expand_grad: float32 [128, 256], P('dp')
All inputs are finite; a program needn't handle non-finite values.
Results may differ from a plain program's by a relative error of at most 0.0069.
Values may be sent and summed in bfloat16 or wider, within the bound.
No kernel may reach another device: no remote copies, remote signals or barrier semaphores. Data moves between devices by JAX's collectives and lax.ppermute only.
A program may use at most 128 MiB of HBM per device.

v0:
```python
import jax
import jax.numpy as jnp
from jax import lax
from jax.sharding import PartitionSpec as P


def extended(block, sides, width):
    for axis, dim in sides:
        count = lax.axis_size(axis)
        forward = [(i, i + 1) for i in range(count - 1)]
        backward = [(target, source) for source, target in forward]
        low = lax.ppermute(
            lax.slice_in_dim(block, block.shape[dim] - width, None, axis=dim), axis, forward
        )
        high = lax.ppermute(lax.slice_in_dim(block, 0, width, axis=dim), axis, backward)
        block = jnp.concatenate([low, block, high], axis=dim)
    return block


def dsilu(value):
    sg = jax.nn.sigmoid(value)
    return sg * (1.0 + value * (1.0 - sg))


def group_conv(inputs, kernel):
    groups = kernel.shape[3] // kernel.shape[2]
    return lax.conv_general_dilated(
        inputs,
        kernel,
        (1, 1),
        ((0, 0), (0, 0)),
        dimension_numbers=("NHWC", "HWIO", "NHWC"),
        feature_group_count=groups,
        preferred_element_type=jnp.float32,
    )


def body(
    features,
    reduce_weight,
    scale_one,
    shift_one,
    group_weight,
    scale_two,
    shift_two,
    expand_weight,
    scale_three,
    shift_three,
    cotangent,
):
    rows = features.shape[1]
    cols = features.shape[2]
    chans = features.shape[3]
    inner = reduce_weight.shape[1]
    group_ch = group_weight.shape[2]
    groups = inner // group_ch
    flat = features.reshape(-1, chans)
    pre_one = (
        jnp.dot(flat, reduce_weight, preferred_element_type=jnp.float32) * scale_one + shift_one
    )
    act_one = jax.nn.silu(pre_one).astype(jnp.bfloat16)
    img_one = act_one.reshape(1, rows, cols, inner)
    padded_act = extended(img_one, (("row", 1), ("col", 2)), 1)
    pre_two = group_conv(padded_act, group_weight).reshape(-1, inner) * scale_two + shift_two
    act_two = jax.nn.silu(pre_two).astype(jnp.bfloat16)
    pre_three = (
        jnp.dot(act_two, expand_weight, preferred_element_type=jnp.float32) * scale_three
        + shift_three
        + flat.astype(jnp.float32)
    )
    back_three = cotangent.reshape(-1, chans).astype(jnp.float32) * dsilu(pre_three)
    grad_three = (back_three * scale_three).astype(jnp.bfloat16)
    gw_three = lax.dot_general(
        act_two, grad_three, (((0,), (0,)), ((), ())), preferred_element_type=jnp.float32
    )
    grad_two = (
        jnp.dot(grad_three, expand_weight.T, preferred_element_type=jnp.float32)
        * dsilu(pre_two)
        * scale_two
    ).astype(jnp.bfloat16)
    padded_grad = extended(grad_two.reshape(1, rows, cols, inner), (("row", 1), ("col", 2)), 1)
    flipped = group_weight[::-1, ::-1].reshape(3, 3, group_ch, groups, group_ch)
    flipped = jnp.transpose(flipped, (0, 1, 4, 3, 2)).reshape(3, 3, group_ch, inner)
    back_one = group_conv(padded_grad, flipped)
    tap_terms = []
    for tap_h in range(3):
        for tap_w in range(3):
            window = padded_act[0, tap_h : tap_h + rows, tap_w : tap_w + cols, :].reshape(-1, inner)
            dense = lax.dot_general(
                window, grad_two, (((0,), (0,)), ((), ())), preferred_element_type=jnp.float32
            )
            blocks = dense.reshape(groups, group_ch, groups, group_ch)
            diag = jnp.diagonal(blocks, axis1=0, axis2=2)
            tap_terms.append(jnp.transpose(diag, (2, 1, 0)).reshape(inner, group_ch))
    gw_two_out = jnp.stack(tap_terms, axis=1).reshape(inner, 3, 3, group_ch)
    grad_one = (back_one.reshape(-1, inner) * dsilu(pre_one) * scale_one).astype(jnp.bfloat16)
    input_grad = (
        jnp.dot(grad_one, reduce_weight.T, preferred_element_type=jnp.float32) + back_three
    ).astype(jnp.bfloat16)
    gw_one = lax.dot_general(
        flat, grad_one, (((0,), (0,)), ((), ())), preferred_element_type=jnp.float32
    )
    summed = lax.psum((gw_one, gw_two_out, gw_three), ("row", "col"))
    shares = (
        lax.psum_scatter(summed[0], "dp", scatter_dimension=0, tiled=True),
        lax.psum_scatter(summed[1], "dp", scatter_dimension=0, tiled=True),
        lax.psum_scatter(summed[2], "dp", scatter_dimension=0, tiled=True),
    )
    total = rows * cols * lax.axis_size("dp") * lax.axis_size("row") * lax.axis_size("col")
    factor = 1.0 / jnp.sqrt(jnp.float32(total))
    return (
        input_grad.reshape(1, rows, cols, chans),
        shares[0] * factor,
        shares[1] * factor,
        shares[2] * factor,
    )


def solution(mesh):
    return jax.shard_map(
        body,
        mesh=mesh,
        in_specs=(
            P("dp", "row", "col", None),
            P(),
            P(),
            P(),
            P(),
            P(),
            P(),
            P(),
            P(),
            P(),
            P("dp", "row", "col", None),
        ),
        out_specs=(
            P("dp", "row", "col", None),
            P("dp", None),
            P("dp", None, None, None),
            P("dp", None),
        ),
        check_vma=False,
    )
```

profile of v0, /device:TPU:8, one launch (start us, length us, event | category | flops | bytes accessed | tf_op | source)
XLA Modules:
  0.0 1005.4 jit_solution(9380093568484053856)
XLA Ops:
  8.0 2.2 multiply_convert_fusion.3
  10.4 1.7 collective-permute-start
  12.1 1.3 collective-permute-start.1
  14.6 1.3 reshape.82
  16.7 3.5 collective-permute-start.2
  20.2 2.4 collective-permute-start.3
  24.8 2.7 collective-permute-done.2
  27.5 3.8 collective-permute-done.3
  31.9 36.1 %copy.89 = bf16[1,10,130,32,4]{4,0,3,2,1:T(2,128)(2,1)} copy(bf16[1,10,130,32,4]{2,4,3,1,0:T(4,128)(2,1)S(1)} %concatenate.46) | data formatting | bytes 665600 | tf_op jit(solution)/shard_map/concatenate | solution.py:16
  68.0 234.4 %convolution_reduce_fusion.1 = f32[8,128,32,4]{3,2,1,0:T(8,128)} fusion(bf16[1,10,130,32,4]{4,0,3,2,1:T(2,128)(2,1)} %copy.89, bf16[3,3,4,32,4]{4,3,2,1,0:T(8,128)(2,1)S(1)} %shard_map.140), kind=kOutput, calls=%fused_computation.10 | convolution fusion | flops 9437184 | bytes 866304 | tf_op jit(solution)/shard_map/conv_general_dilated | solution.py:27
  302.5 14.9 %reshape.158 = f32[1024,128]{1,0:T(8,128)S(1)} reshape(f32[8,128,32,4]{3,2,1,0:T(8,128)} %convolution_reduce_fusion.1) | data formatting | bytes 1048576 | tf_op jit(solution)/shard_map/reshape | solution.py:64
  322.8 1.9 copy.104
  327.6 2.1 convolution_bitcast_fusion.6
  329.7 1.9 copy.110
  335.1 2.1 convolution_bitcast_fusion.5
  337.2 1.9 copy.115
  341.7 1.3 convolution_bitcast_fusion.4
  344.8 2.2 reshape.85
  347.0 3.2 copy.242
  350.2 2.3 gather_fusion.4
  365.1 3.2 collective-permute-start.4
  378.6 3.5 collective-permute-start.6
  382.1 2.4 collective-permute-start.7
  384.5 1.7 fusion.24
  386.3 3.9 collective-permute-done.6
  390.2 3.8 collective-permute-done.7
  394.6 36.1 %copy.96 = bf16[1,10,130,32,4]{4,0,3,2,1:T(2,128)(2,1)} copy(bf16[1,10,130,32,4]{2,4,3,1,0:T(4,128)(2,1)S(1)} %concatenate.49) | data formatting | bytes 665600 | tf_op jit(solution)/shard_map/concatenate | solution.py:16
  430.7 398.5 %convolution_reduce_fusion = f32[8,128,32,4]{3,2,1,0:T(8,128)} fusion(bf16[1,10,130,32,4]{4,0,3,2,1:T(2,128)(2,1)} %copy.96, bf16[3,3,4,32,4]{4,3,2,1,0:T(8,128)(2,1)S(1)} %copy-done.22), kind=kOutput, calls=%fused_computation.9 | convolution fusion | flops 9437184 | bytes 866304 | tf_op jit(solution)/shard_map/conv_general_dilated | solution.py:27
  829.3 14.9 %reshape.159 = f32[1024,128]{1,0:T(8,128)S(1)} reshape(f32[8,128,32,4]{3,2,1,0:T(8,128)} %convolution_reduce_fusion) | data formatting | bytes 1048576 | tf_op jit(solution)/shard_map/reshape | solution.py:96
  847.6 56.6 %psum.25 = f32[64,3,3,4]{0,3,2,1:T(4,128)S(1)} all-reduce(f32[64,3,3,4]{0,3,2,1:T(4,128)S(1)} %copy.175), channel_id=1, replica_groups=mesh['dp'=2,'row'=4,'col'=4] {'row','col'}, use_global_device_ids=true, to_apply=%region_2.3 | all-reduce | flops 2304 | bytes 18432 | tf_op jit(solution)/shard_map/psum | solution.py:103
  904.9 90.5 %all-reduce.3.cloned.1.call-done = (f32[128,128]{0,1:T(8,128)}, f32[64,256]{1,0:T(8,128)}) async-done(((f32[128,128]{0,1:T(8,128)}, f32[64,256]{1,0:T(8,128)}), (f32[128,128]{0,1:T(8,128)}, f32[64,256]{1,0:T(8,128)})) %all-reduce.3.cloned.1.call-update) | async-done | bytes 131088 | tf_op jit(solution)/shard_map/psum | solution.py:103
  996.9 1.5 broadcast_multiply_fusion
  (186 shorter events, 50.8 us)
Async XLA Ops:
  7.2 6.8 copy-start.26
  7.2 839.3 %reduce-scatter.10.cloned.1.call-start = ((), (), s32[]{:S(2)}) async-start(), calls=%async_computation.5 | async-start | bytes 98304
  10.2 12.7 %copy-start.4 = (bf16[1024,128]{1,0:T(8,128)(2,1)}, bf16[1024,128]{1,0:T(8,128)(2,1)S(1)}, u32[]{:S(2)}) copy-start(bf16[1024,128]{1,0:T(8,128)(2,1)S(1)} %get-tuple-element.36) | copy-start | bytes 786436
  10.4 20.9 %copy-start.2 = (bf16[1,8,128,128]{2,3,1,0:T(8,128)(2,1)}, bf16[1,8,128,128]{2,3,1,0:T(8,128)(2,1)S(1)}, u32[]{:S(2)}) copy-start(bf16[1,8,128,128]{2,3,1,0:T(8,128)(2,1)S(1)} %copy.86) | copy-start | bytes 786436
  10.4 5.5 collective-permute-start
  12.1 4.4 collective-permute-start.1
  15.9 15.3 %copy-start.13 = (bf16[1,1,128,128]{2,3,1,0:T(8,128)(2,1)}, bf16[1,1,128,128]{2,3,1,0:T(8,128)(2,1)S(1)}, u32[]{:S(2)}) copy-start(bf16[1,1,128,128]{2,3,1,0:T(8,128)(2,1)S(1)} %collective-permute-done) | copy-start | bytes 98308
  16.5 14.8 %copy-start.15 = (bf16[1,1,128,128]{2,3,1,0:T(8,128)(2,1)}, bf16[1,1,128,128]{2,3,1,0:T(8,128)(2,1)S(1)}, u32[]{:S(2)}) copy-start(bf16[1,1,128,128]{2,3,1,0:T(8,128)(2,1)S(1)} %collective-permute-done.1) | copy-start | bytes 98308
  16.7 10.8 %collective-permute-start.2 = (bf16[1,10,1,128]{2,3,1,0:T(8,128)(2,1)S(1)}, bf16[1,10,1,128]{2,3,1,0:T(8,128)(2,1)S(1)}, u32[]{:S(2)}, u32[]{:S(2)}) collective-permute-start(bf16[1,10,1,128]{2,3,1,0:T(8,128)(2,1)S(1)} %get-tuple-element.28), channel_id=1, source_target_pairs={{0,1},{1,2},{2,3},{4,5},{5,6},{6,7},{8,9},{9,10},{10,11},{12,13},{... | collective-permute-start | bytes 7688 | tf_op jit(solution)/shard_map/ppermute | solution.py:12
  20.2 11.0 %collective-permute-start.3 = (bf16[1,10,1,128]{2,3,1,0:T(8,128)(2,1)S(1)}, bf16[1,10,1,128]{2,3,1,0:T(8,128)(2,1)S(1)}, u32[]{:S(2)}, u32[]{:S(2)}) collective-permute-start(bf16[1,10,1,128]{2,3,1,0:T(8,128)(2,1)S(1)} %get-tuple-element.29), channel_id=1, source_target_pairs={{1,0},{2,1},{3,2},{5,4},{6,5},{7,6},{9,8},{10,9},{11,10},{13,12},{... | collective-permute-start | bytes 7688 | tf_op jit(solution)/shard_map/ppermute | solution.py:15
  27.5 40.5 %copy-start.6 = (bf16[1,10,1,128]{2,3,1,0:T(8,128)(2,1)}, bf16[1,10,1,128]{2,3,1,0:T(8,128)(2,1)S(1)}, u32[]{:S(2)}) copy-start(bf16[1,10,1,128]{2,3,1,0:T(8,128)(2,1)S(1)} %collective-permute-done.2) | copy-start | bytes 7684
  31.3 36.7 %copy-start.8 = (bf16[1,10,1,128]{2,3,1,0:T(8,128)(2,1)}, bf16[1,10,1,128]{2,3,1,0:T(8,128)(2,1)S(1)}, u32[]{:S(2)}) copy-start(bf16[1,10,1,128]{2,3,1,0:T(8,128)(2,1)S(1)} %collective-permute-done.3) | copy-start | bytes 7684
  302.4 14.9 %copy-start.20 = (bf16[1,8,128,256]{3,2,1,0:T(8,128)(2,1)S(1)}, bf16[1,8,128,256]{3,2,1,0:T(8,128)(2,1)}, u32[]{:S(2)}) copy-start(bf16[1,8,128,256]{3,2,1,0:T(8,128)(2,1)} %param.11) | copy-start | bytes 1572868
  302.4 14.9 %copy-start.28 = (bf16[1,8,128,256]{3,2,1,0:T(8,128)(2,1)S(1)}, bf16[1,8,128,256]{3,2,1,0:T(8,128)(2,1)}, u32[]{:S(2)}) copy-start(bf16[1,8,128,256]{3,2,1,0:T(8,128)(2,1)} %param.21) | copy-start | bytes 1572868
  302.4 14.9 %copy-start.29 = (bf16[128,256]{1,0:T(8,128)(2,1)S(1)}, bf16[128,256]{1,0:T(8,128)(2,1)}, u32[]{:S(2)}) copy-start(bf16[128,256]{1,0:T(8,128)(2,1)} %param.18) | copy-start | bytes 196612
  302.4 14.9 %copy-start.30 = (f32[256]{0:T(256)S(1)}, f32[256]{0:T(256)}, u32[]{:S(2)}) copy-start(f32[256]{0:T(256)} %param.20) | copy-start | bytes 3076
  302.4 15.0 %copy-start.31 = (f32[256]{0:T(256)S(1)}, f32[256]{0:T(256)}, u32[]{:S(2)}) copy-start(f32[256]{0:T(256)} %param.19) | copy-start | bytes 3076
  302.4 15.0 %copy-start.32 = (f32[128]{0:T(128)S(1)}, f32[128]{0:T(128)}, u32[]{:S(2)}) copy-start(f32[128]{0:T(128)} %param.17) | copy-start | bytes 1540
  302.5 15.0 %copy-start.33 = (f32[128]{0:T(128)S(1)}, f32[128]{0:T(128)}, u32[]{:S(2)}) copy-start(f32[128]{0:T(128)} %param.16) | copy-start | bytes 1540
  364.1 20.4 %copy-start.11 = (f32[1024,256]{1,0:T(8,128)S(1)}, f32[1024,256]{1,0:T(8,128)}, u32[]{:S(2)}) copy-start(f32[1024,256]{1,0:T(8,128)} %copy-done.10) | copy-start | bytes 3145732
  364.8 19.8 %copy-start.19 = (f32[1024,128]{1,0:T(8,128)S(1)}, f32[1024,128]{1,0:T(8,128)}, u32[]{:S(2)}) copy-start(f32[1024,128]{1,0:T(8,128)} %copy-done.18) | copy-start | bytes 1572868
  365.1 13.3 %collective-permute-start.4 = (bf16[1,1,128,128]{2,3,1,0:T(8,128)(2,1)S(1)}, bf16[1,1,128,128]{2,3,1,0:T(8,128)(2,1)S(1)}, u32[]{:S(2)}, u32[]{:S(2)}) collective-permute-start(bf16[1,1,128,128]{2,3,1,0:T(8,128)(2,1)S(1)} %get-tuple-element.32), channel_id=1, source_target_pairs={{0,4},{4,8},{8,12},{1,5},{5,9},{9,13},{2,6},{6,10},{10,14},{3,7},{... | collective-permute-start | bytes 98312 | tf_op jit(solution)/shard_map/ppermute | solution.py:12
  368.3 10.1 %collective-permute-start.5 = (bf16[1,1,128,128]{2,3,1,0:T(8,128)(2,1)S(1)}, bf16[1,1,128,128]{2,3,1,0:T(8,128)(2,1)S(1)}, u32[]{:S(2)}, u32[]{:S(2)}) collective-permute-start(bf16[1,1,128,128]{2,3,1,0:T(8,128)(2,1)S(1)} %get-tuple-element.33), channel_id=1, source_target_pairs={{4,0},{8,4},{12,8},{5,1},{9,5},{13,9},{6,2},{10,6},{14,10},{7,3},{... | collective-permute-start | bytes 98312 | tf_op jit(solution)/shard_map/ppermute | solution.py:15
  378.3 525.9 %reduce-scatter.8.cloned.1.call-start = ((), (), s32[]{:S(2)}) async-start(), calls=%async_computation.4 | async-start | bytes 196608 | tf_op jit(solution)/shard_map/reduce_scatter | solution.py:107
  378.6 11.5 %collective-permute-start.6 = (bf16[1,10,1,128]{2,3,1,0:T(8,128)(2,1)S(1)}, bf16[1,10,1,128]{2,3,1,0:T(8,128)(2,1)S(1)}, u32[]{:S(2)}, u32[]{:S(2)}) collective-permute-start(bf16[1,10,1,128]{2,3,1,0:T(8,128)(2,1)S(1)} %get-tuple-element.26), channel_id=1, source_target_pairs={{0,1},{1,2},{2,3},{4,5},{5,6},{6,7},{8,9},{9,10},{10,11},{12,13},{... | collective-permute-start | bytes 7688 | tf_op jit(solution)/shard_map/ppermute | solution.py:12
  382.1 11.9 %collective-permute-start.7 = (bf16[1,10,1,128]{2,3,1,0:T(8,128)(2,1)S(1)}, bf16[1,10,1,128]{2,3,1,0:T(8,128)(2,1)S(1)}, u32[]{:S(2)}, u32[]{:S(2)}) collective-permute-start(bf16[1,10,1,128]{2,3,1,0:T(8,128)(2,1)S(1)} %get-tuple-element.27), channel_id=1, source_target_pairs={{1,0},{2,1},{3,2},{5,4},{6,5},{7,6},{9,8},{10,9},{11,10},{13,12},{... | collective-permute-start | bytes 7688 | tf_op jit(solution)/shard_map/ppermute | solution.py:15
  386.3 518.0 %reduce-scatter.6.cloned.1.call-start = ((), (), s32[]{:S(2)}) async-start(), calls=%async_computation.3 | async-start | bytes 196608 | tf_op jit(solution)/shard_map/reduce_scatter | solution.py:105
  394.6 36.1 %copy-start.22 = (bf16[3,3,4,32,4]{4,3,2,1,0:T(8,128)(2,1)S(1)}, bf16[3,3,4,32,4]{4,3,2,1,0:T(8,128)(2,1)}, u32[]{:S(2)}) copy-start(bf16[3,3,4,32,4]{4,3,2,1,0:T(8,128)(2,1)} %reshape.82) | copy-start | bytes 27652
  829.2 14.9 %copy-start.17 = (f32[1024,128]{1,0:T(8,128)S(1)}, f32[1024,128]{1,0:T(8,128)}, u32[]{:S(2)}) copy-start(f32[1024,128]{1,0:T(8,128)} %get-tuple-element.37) | copy-start | bytes 1572868
  829.3 14.9 %copy-start.27 = (f32[128]{0:T(128)S(1)}, f32[128]{0:T(128)}, u32[]{:S(2)}) copy-start(f32[128]{0:T(128)} %param.13) | copy-start | bytes 1540
  829.3 15.1 %copy-start.21 = (bf16[1,8,128,256]{3,2,1,0:T(8,128)(2,1)S(1)}, bf16[1,8,128,256]{3,2,1,0:T(8,128)(2,1)}, u32[]{:S(2)}) copy-start(bf16[1,8,128,256]{3,2,1,0:T(8,128)(2,1)} %param.11) | copy-start | bytes 1572868
  845.3 150.0 %all-reduce.3.cloned.1.call-start = ((), (), s32[]{:S(2)}) async-start(), calls=%async_computation.6 | async-start | bytes 262144 | tf_op jit(solution)/shard_map/psum | solution.py:103
  (14 other events, 28.2 us)
Sparse Core Ops, SparseCore 0:
  378.5 12.0 reduce-scatter.9
  392.8 10.2 reduce-scatter.7
  845.4 9.5 reduce-scatter.5
  904.4 90.9 all-reduce.2
where the time goes:
time: 1010 us
  matrix products  648 us (64%)
  local copies, waits for them, and re-layouts  156 us (15%)
  waiting for transfers between devices  105 us (10%)
  blocking collectives  56.6 us (6%)
  starting transfers between devices  19.4 us (2%)
  between operations  15.1 us (1%)
    conv_general_dilated x2, matrix products, group_conv(): lax.conv_general_dilated(inputs, kernel, (1, 1), ((0, 0), (0, 0)), dimens...  633 us
    psum x1, waiting for transfers between devices, body(): summed = lax.psum((gw_one, gw_two_out, gw_three), ('row', 'col'))  90.5 us
    concatenate x4, local copies, waits for them, and re-layouts, extended(): block = jnp.concatenate([low, block, high], axis=dim)  72.6 us
    psum x1, blocking collectives, body(): summed = lax.psum((gw_one, gw_two_out, gw_three), ('row', 'col'))  56.6 us
  transfers between devices with their start and end apart: 12, of which 6 were waited for; matrix products, arithmetic and copies ran while one was open for 47% of the time, Pallas kernels for 0%

commit v1 on v0

--- a/solution.py
+++ b/solution.py
@@ -100,7 +100,8 @@
     gw_one = lax.dot_general(
         flat, grad_one, (((0,), (0,)), ((), ())), preferred_element_type=jnp.float32
     )
-    summed = lax.psum((gw_one, gw_two_out, gw_three), ("row", "col"))
+    one_axis = lax.psum((gw_one, gw_two_out, gw_three), "col")
+    summed = lax.psum(one_axis, "row")
     shares = (
         lax.psum_scatter(summed[0], "dp", scatter_dimension=0, tiled=True),
         lax.psum_scatter(summed[1], "dp", scatter_dimension=0, tiled=True),

time: 1010 us -> 944 us (0.935)
  waiting for transfers between devices: 105 us -> 69.3 us
  blocking collectives: 56.6 us -> 25.6 us
    psum x1 -> x2, waiting for transfers between devices: 90.5 us -> 43.1 us  [the longest x1 33.1 us: body(): summed = lax.psum(one_axis, 'row')]
    psum x1 -> x2, blocking collectives: 56.6 us -> 25.6 us  [the longest x1 15.4 us: body(): one_axis = lax.psum((gw_one, gw_two_out, gw_three), 'col')]
    unnamed x5 -> x6, waiting for transfers between devices: 0.07 us -> 11.6 us
  transfers between devices with their start and end apart: 12 -> 13, of which waited for: 6 -> 9; matrix products, arithmetic and copies ran while one was open for 47% -> 51% of each run, Pallas kernels for 0% -> 0%
where the time goes in v1:
time: 944 us; the launch traced here: 938 us
  matrix products  650 us (69%)
  local copies, waits for them, and re-layouts  153 us (16%)
  waiting for transfers between devices  69.3 us (7%)
  blocking collectives  25.6 us (3%)
  starting transfers between devices  19.4 us (2%)
  between operations  14.8 us (2%)
    conv_general_dilated x2, matrix products, group_conv(): lax.conv_general_dilated(inputs, kernel, (1, 1), ((0, 0), (0, 0)), dimens...  633 us
    concatenate x4, local copies, waits for them, and re-layouts, extended(): block = jnp.concatenate([low, block, high], axis=dim)  72.6 us
    psum x1, waiting for transfers between devices, body(): summed = lax.psum(one_axis, 'row')  33.1 us
  transfers between devices with their start and end apart: 13, of which 9 were waited for; matrix products, arithmetic and copies ran while one was open for 51% of the time, Pallas kernels for 0%

profile of v1, /device:TPU:8, one launch (start us, length us, event | category | flops | bytes accessed | tf_op | source)
XLA Modules:
  0.0 938.1 jit_solution(8892262451598347505)
XLA Ops:
  8.0 2.1 multiply_convert_fusion.3
  10.4 1.7 collective-permute-start
  16.7 3.5 collective-permute-start.2
  20.2 2.4 collective-permute-start.3
  24.8 2.7 collective-permute-done.2
  27.5 3.8 collective-permute-done.3
  31.9 36.1 %copy.89 = bf16[1,10,130,32,4]{4,0,3,2,1:T(2,128)(2,1)} copy(bf16[1,10,130,32,4]{2,4,3,1,0:T(4,128)(2,1)S(1)} %concatenate.46) | data formatting | bytes 665600 | tf_op jit(solution)/shard_map/concatenate | solution.py:16
  68.0 234.5 %convolution_reduce_fusion.1 = f32[8,128,32,4]{3,2,1,0:T(8,128)} fusion(bf16[1,10,130,32,4]{4,0,3,2,1:T(2,128)(2,1)} %copy.89, bf16[3,3,4,32,4]{4,3,2,1,0:T(8,128)(2,1)S(1)} %shard_map.140), kind=kOutput, calls=%fused_computation.10 | convolution fusion | flops 9437184 | bytes 866304 | tf_op jit(solution)/shard_map/conv_general_dilated | solution.py:27
  302.6 14.9 %reshape.158 = f32[1024,128]{1,0:T(8,128)S(1)} reshape(f32[8,128,32,4]{3,2,1,0:T(8,128)} %convolution_reduce_fusion.1) | data formatting | bytes 1048576 | tf_op jit(solution)/shard_map/reshape | solution.py:64
  323.8 1.9 copy.104
  328.5 2.1 convolution_bitcast_fusion.6
  330.6 1.9 copy.110
  336.0 2.1 convolution_bitcast_fusion.5
  338.1 1.9 copy.115
  345.9 2.2 reshape.85
  348.1 3.2 copy.242
  351.3 2.3 gather_fusion.4
  358.6 3.2 collective-permute-start.4
  367.4 3.5 collective-permute-start.6
  370.9 2.4 collective-permute-start.7
  373.9 1.9 copy.132
  378.9 3.9 collective-permute-done.7
  384.4 36.1 %copy.96 = bf16[1,10,130,32,4]{4,0,3,2,1:T(2,128)(2,1)} copy(bf16[1,10,130,32,4]{2,4,3,1,0:T(4,128)(2,1)S(1)} %concatenate.49) | data formatting | bytes 665600 | tf_op jit(solution)/shard_map/concatenate | solution.py:16
  420.5 398.6 %convolution_reduce_fusion = f32[8,128,32,4]{3,2,1,0:T(8,128)} fusion(bf16[1,10,130,32,4]{4,0,3,2,1:T(2,128)(2,1)} %copy.96, bf16[3,3,4,32,4]{4,3,2,1,0:T(8,128)(2,1)S(1)} %copy-done.20), kind=kOutput, calls=%fused_computation.9 | convolution fusion | flops 9437184 | bytes 866304 | tf_op jit(solution)/shard_map/conv_general_dilated | solution.py:27
  819.1 14.9 %reshape.159 = f32[1024,128]{1,0:T(8,128)S(1)} reshape(f32[8,128,32,4]{3,2,1,0:T(8,128)} %convolution_reduce_fusion) | data formatting | bytes 1048576 | tf_op jit(solution)/shard_map/reshape | solution.py:96
  837.7 1.9 copy.143
  843.1 2.0 reduce-scatter.6.cloned.1.call-done
  846.3 11.5 %reduce-scatter.10.cloned.1.call-done = f32[64,36]{1,0:T(8,128)} async-done(((f32[128,36]{1,0:T(8,128)}), f32[64,36]{1,0:T(8,128)}) %reduce-scatter.10.cloned.1.call-update) | async-done | bytes 9232
  858.9 15.4 %psum.52 = f32[64,3,3,4]{0,3,2,1:T(4,128)S(1)} all-reduce(f32[64,3,3,4]{0,3,2,1:T(4,128)S(1)} %copy.175), channel_id=1, replica_groups=mesh['dp'=2,'row'=4,'col'=4] {'col'}, use_global_device_ids=true, to_apply=%region_3.4 | all-reduce | flops 2304 | bytes 18432 | tf_op jit(solution)/shard_map/psum | solution.py:103
  874.3 10.2 %psum.49 = f32[64,3,3,4]{0,3,2,1:T(4,128)S(1)} all-reduce(f32[64,3,3,4]{0,3,2,1:T(4,128)S(1)} %psum.52), channel_id=1, replica_groups=mesh['dp'=2,'row'=4,'col'=4] {'row'}, use_global_device_ids=true, to_apply=%region_4.5 | all-reduce | flops 2304 | bytes 18432 | tf_op jit(solution)/shard_map/psum | solution.py:104
  884.5 10.1 %all-reduce.5.cloned.1.call-done = (f32[128,128]{0,1:T(8,128)}, f32[64,256]{1,0:T(8,128)}) async-done(((f32[128,128]{0,1:T(8,128)}, f32[64,256]{1,0:T(8,128)}), (f32[128,128]{0,1:T(8,128)}, f32[64,256]{1,0:T(8,128)})) %all-reduce.5.cloned.1.call-update) | async-done | bytes 131088 | tf_op jit(solution)/shard_map/psum | solution.py:103
  895.2 33.1 %all-reduce.7.cloned.1.call-done = (f32[128,128]{0,1:T(8,128)}, f32[64,256]{1,0:T(8,128)}) async-done(((f32[128,128]{0,1:T(8,128)}, f32[64,256]{1,0:T(8,128)}), (f32[128,128]{0,1:T(8,128)}, f32[64,256]{1,0:T(8,128)})) %all-reduce.7.cloned.1.call-update) | async-done | bytes 131088 | tf_op jit(solution)/shard_map/psum | solution.py:104
  (190 shorter events, 55.5 us)
Async XLA Ops:
  7.2 6.8 copy-start.25
  7.2 835.9 %reduce-scatter.8.cloned.1.call-start = ((), (), s32[]{:S(2)}) async-start(), calls=%async_computation.4 | async-start | bytes 196608 | tf_op jit(solution)/shard_map/reduce_scatter | solution.py:108
  10.2 12.7 %copy-start.5 = (bf16[1024,128]{1,0:T(8,128)(2,1)}, bf16[1024,128]{1,0:T(8,128)(2,1)S(1)}, u32[]{:S(2)}) copy-start(bf16[1024,128]{1,0:T(8,128)(2,1)S(1)} %get-tuple-element.38) | copy-start | bytes 786436
  10.3 20.9 %copy-start.3 = (bf16[1,8,128,128]{2,3,1,0:T(8,128)(2,1)}, bf16[1,8,128,128]{2,3,1,0:T(8,128)(2,1)S(1)}, u32[]{:S(2)}) copy-start(bf16[1,8,128,128]{2,3,1,0:T(8,128)(2,1)S(1)} %copy.86) | copy-start | bytes 786436
  10.4 5.6 collective-permute-start
  12.1 4.4 collective-permute-start.1
  16.0 15.3 %copy-start.13 = (bf16[1,1,128,128]{2,3,1,0:T(8,128)(2,1)}, bf16[1,1,128,128]{2,3,1,0:T(8,128)(2,1)S(1)}, u32[]{:S(2)}) copy-start(bf16[1,1,128,128]{2,3,1,0:T(8,128)(2,1)S(1)} %collective-permute-done) | copy-start | bytes 98308
  16.5 14.8 %copy-start.15 = (bf16[1,1,128,128]{2,3,1,0:T(8,128)(2,1)}, bf16[1,1,128,128]{2,3,1,0:T(8,128)(2,1)S(1)}, u32[]{:S(2)}) copy-start(bf16[1,1,128,128]{2,3,1,0:T(8,128)(2,1)S(1)} %collective-permute-done.1) | copy-start | bytes 98308
  16.7 10.8 %collective-permute-start.2 = (bf16[1,10,1,128]{2,3,1,0:T(8,128)(2,1)S(1)}, bf16[1,10,1,128]{2,3,1,0:T(8,128)(2,1)S(1)}, u32[]{:S(2)}, u32[]{:S(2)}) collective-permute-start(bf16[1,10,1,128]{2,3,1,0:T(8,128)(2,1)S(1)} %get-tuple-element.30), channel_id=1, source_target_pairs={{0,1},{1,2},{2,3},{4,5},{5,6},{6,7},{8,9},{9,10},{10,11},{12,13},{... | collective-permute-start | bytes 7688 | tf_op jit(solution)/shard_map/ppermute | solution.py:12
  20.2 11.0 %collective-permute-start.3 = (bf16[1,10,1,128]{2,3,1,0:T(8,128)(2,1)S(1)}, bf16[1,10,1,128]{2,3,1,0:T(8,128)(2,1)S(1)}, u32[]{:S(2)}, u32[]{:S(2)}) collective-permute-start(bf16[1,10,1,128]{2,3,1,0:T(8,128)(2,1)S(1)} %get-tuple-element.31), channel_id=1, source_target_pairs={{1,0},{2,1},{3,2},{5,4},{6,5},{7,6},{9,8},{10,9},{11,10},{13,12},{... | collective-permute-start | bytes 7688 | tf_op jit(solution)/shard_map/ppermute | solution.py:15
  27.5 40.5 %copy-start.7 = (bf16[1,10,1,128]{2,3,1,0:T(8,128)(2,1)}, bf16[1,10,1,128]{2,3,1,0:T(8,128)(2,1)S(1)}, u32[]{:S(2)}) copy-start(bf16[1,10,1,128]{2,3,1,0:T(8,128)(2,1)S(1)} %collective-permute-done.2) | copy-start | bytes 7684
  31.3 36.7 %copy-start.9 = (bf16[1,10,1,128]{2,3,1,0:T(8,128)(2,1)}, bf16[1,10,1,128]{2,3,1,0:T(8,128)(2,1)S(1)}, u32[]{:S(2)}) copy-start(bf16[1,10,1,128]{2,3,1,0:T(8,128)(2,1)S(1)} %collective-permute-done.3) | copy-start | bytes 7684
  302.6 14.9 %copy-start.18 = (bf16[1,8,128,256]{3,2,1,0:T(8,128)(2,1)S(1)}, bf16[1,8,128,256]{3,2,1,0:T(8,128)(2,1)}, u32[]{:S(2)}) copy-start(bf16[1,8,128,256]{3,2,1,0:T(8,128)(2,1)} %param.11) | copy-start | bytes 1572868
  302.6 14.9 %copy-start.28 = (bf16[1,8,128,256]{3,2,1,0:T(8,128)(2,1)S(1)}, bf16[1,8,128,256]{3,2,1,0:T(8,128)(2,1)}, u32[]{:S(2)}) copy-start(bf16[1,8,128,256]{3,2,1,0:T(8,128)(2,1)} %param.21) | copy-start | bytes 1572868
  302.6 14.9 %copy-start.29 = (bf16[128,256]{1,0:T(8,128)(2,1)S(1)}, bf16[128,256]{1,0:T(8,128)(2,1)}, u32[]{:S(2)}) copy-start(bf16[128,256]{1,0:T(8,128)(2,1)} %param.18) | copy-start | bytes 196612
  302.6 14.9 %copy-start.30 = (f32[256]{0:T(256)S(1)}, f32[256]{0:T(256)}, u32[]{:S(2)}) copy-start(f32[256]{0:T(256)} %param.20) | copy-start | bytes 3076
  302.6 14.9 %copy-start.31 = (f32[256]{0:T(256)S(1)}, f32[256]{0:T(256)}, u32[]{:S(2)}) copy-start(f32[256]{0:T(256)} %param.19) | copy-start | bytes 3076
  302.6 14.9 %copy-start.32 = (f32[128]{0:T(128)S(1)}, f32[128]{0:T(128)}, u32[]{:S(2)}) copy-start(f32[128]{0:T(128)} %param.17) | copy-start | bytes 1540
  302.6 14.9 %copy-start.33 = (f32[128]{0:T(128)S(1)}, f32[128]{0:T(128)}, u32[]{:S(2)}) copy-start(f32[128]{0:T(128)} %param.16) | copy-start | bytes 1540
  358.6 8.6 collective-permute-start.4
  361.7 5.4 collective-permute-start.5
  367.4 11.5 %collective-permute-start.6 = (bf16[1,10,1,128]{2,3,1,0:T(8,128)(2,1)S(1)}, bf16[1,10,1,128]{2,3,1,0:T(8,128)(2,1)S(1)}, u32[]{:S(2)}, u32[]{:S(2)}) collective-permute-start(bf16[1,10,1,128]{2,3,1,0:T(8,128)(2,1)S(1)} %get-tuple-element.28), channel_id=1, source_target_pairs={{0,1},{1,2},{2,3},{4,5},{5,6},{6,7},{8,9},{9,10},{10,11},{12,13},{... | collective-permute-start | bytes 7688 | tf_op jit(solution)/shard_map/ppermute | solution.py:12
  370.9 11.9 %collective-permute-start.7 = (bf16[1,10,1,128]{2,3,1,0:T(8,128)(2,1)S(1)}, bf16[1,10,1,128]{2,3,1,0:T(8,128)(2,1)}, u32[]{:S(2)}, u32[]{:S(2)}) collective-permute-start(bf16[1,10,1,128]{2,3,1,0:T(8,128)(2,1)S(1)} %get-tuple-element.29), channel_id=1, source_target_pairs={{1,0},{2,1},{3,2},{5,4},{6,5},{7,6},{9,8},{10,9},{11,10},{13,12},{... | collective-permute-start | bytes 7688 | tf_op jit(solution)/shard_map/ppermute | solution.py:15
  377.2 467.9 %reduce-scatter.6.cloned.1.call-start = ((), (), s32[]{:S(2)}) async-start(), calls=%async_computation.3 | async-start | bytes 196608 | tf_op jit(solution)/shard_map/reduce_scatter | solution.py:106
  384.3 36.1 %copy-start.20 = (bf16[3,3,4,32,4]{4,3,2,1,0:T(8,128)(2,1)S(1)}, bf16[3,3,4,32,4]{4,3,2,1,0:T(8,128)(2,1)}, u32[]{:S(2)}) copy-start(bf16[3,3,4,32,4]{4,3,2,1,0:T(8,128)(2,1)} %reshape.82) | copy-start | bytes 27652
  819.1 14.9 %copy-start.17 = (f32[1024,128]{1,0:T(8,128)S(1)}, f32[1024,128]{1,0:T(8,128)}, u32[]{:S(2)}) copy-start(f32[1024,128]{1,0:T(8,128)} %get-tuple-element.39) | copy-start | bytes 1572868
  819.1 14.9 %copy-start.27 = (f32[128]{0:T(128)S(1)}, f32[128]{0:T(128)}, u32[]{:S(2)}) copy-start(f32[128]{0:T(128)} %param.13) | copy-start | bytes 1540
  819.1 15.1 %copy-start.19 = (bf16[1,8,128,256]{3,2,1,0:T(8,128)(2,1)S(1)}, bf16[1,8,128,256]{3,2,1,0:T(8,128)(2,1)}, u32[]{:S(2)}) copy-start(bf16[1,8,128,256]{3,2,1,0:T(8,128)(2,1)} %param.11) | copy-start | bytes 1572868
  835.2 22.6 %reduce-scatter.10.cloned.1.call-start = ((), (), s32[]{:S(2)}) async-start(), calls=%async_computation.5 | async-start | bytes 98304
  836.9 8.3 copy-start.12
  843.0 51.5 %all-reduce.5.cloned.1.call-start = ((), (), s32[]{:S(2)}) async-start(), calls=%async_computation.6 | async-start | bytes 262144 | tf_op jit(solution)/shard_map/psum | solution.py:103
  845.1 83.2 %all-reduce.7.cloned.1.call-start = ((), (), s32[]{:S(2)}) async-start(), calls=%async_computation.7 | async-start | bytes 262144 | tf_op jit(solution)/shard_map/psum | solution.py:104
  (15 other events, 29.9 us)
Sparse Core Ops, SparseCore 0:
  377.3 12.7 reduce-scatter.7
  835.3 9.7 reduce-scatter.5
  847.9 9.8 reduce-scatter.9
  860.0 34.5 all-reduce.4
  896.9 31.3 all-reduce.6
